TPU v7x, 512 devices: a whole 4x8x8 slice. The times are simulated.
512 devices in a mesh: sx: 8 (over x, core), sy: 8 (over z), dir: 8 (over y).
Axes of the slice: x: 4, y: 8, z: 8, core: 2. Of those that a mesh axis runs over, the one named last changes fastest.
Arguments:
- directions: float32 [7, 64, 16, 64, 128], P(None, 'dir', 'sx', 'sy'), may hold values from -6 to 6
- conductance: float32 [7, 16, 64, 128], P(None, 'sx', 'sy'), may hold values from 0.2 to 0.4
- diag_inverse: float32 [7, 16, 64, 128], P(None, 'sx', 'sy'), may hold values from 0.3 to 0.9
- cross_inverse: float32 [7, 7, 16, 64, 128], P(None, None, 'sx', 'sy'), may hold values from -0.5 to 0.5
- coupling: int32 [7, 7], replicated, may hold values 0 or 1
- sensitivity: float32 [7, 16, 64, 128], P(None, 'sx', 'sy'), may hold values from -6 to 6
- obs_weight: float32 [7, 16, 64, 128], P(None, 'sx', 'sy'), may hold values from 0.3 to 3
- prior_weight: float32 [7, 16, 64, 128], P(None, 'sx', 'sy'), may hold values from 0.1 to 0.5
Outputs:
- hess_action: float32 [7, 64, 16, 64, 128], P(None, 'dir', 'sx', 'sy')
- r_factor: float32 [64, 64], replicated
All inputs are finite; a program needn't handle non-finite values.
Results may differ from a plain program's by a relative error of at most 0.0002.
Values sent between devices are 32-bit elements; how exact they have to be, the bound alone decides.
No kernel may reach another device: no remote copies, remote signals or barrier semaphores. Data moves between devices by JAX's collectives and lax.ppermute only.
A program may use at most 64 MiB of HBM per device.

v0:
```python
import jax
import jax.numpy as jnp
from jax import lax
from jax.sharding import PartitionSpec as P

SWEEPS = 4


def with_halo(cells, sides, width, closed):
    for axis, dim in sides:
        count = lax.axis_size(axis)
        ends = count if closed else count - 1
        head = lax.slice_in_dim(cells, 0, width, axis=dim)
        tail = lax.slice_in_dim(cells, cells.shape[dim] - width, cells.shape[dim], axis=dim)
        cells = jnp.concatenate(
            [
                lax.ppermute(tail, axis, [(i, (i + 1) % count) for i in range(ends)]),
                cells,
                lax.ppermute(head, axis, [((i + 1) % count, i) for i in range(ends)]),
            ],
            axis=dim,
        )
    return cells


def apply_block(diag_inverse, cross_eff, source, transpose):
    result = diag_inverse[:, None] * source
    for species in range(source.shape[0]):
        column = cross_eff[species] if transpose else cross_eff[:, species]
        result = result + column[:, None] * source[species][None]
    return result


def neighbour_parts(centre, wide_x, wide_y):
    zeros_z = jnp.zeros_like(centre[..., :1])
    forward_z = jnp.concatenate([centre[..., 1:], zeros_z], axis=-1)
    backward_z = jnp.concatenate([zeros_z, centre[..., :-1]], axis=-1)
    return (
        wide_x[..., 2:, :, :]
        + wide_x[..., :-2, :, :]
        + wide_y[..., 2:, :]
        + wide_y[..., :-2, :]
        + forward_z
        + backward_z
    )


def jacobi_single(rhs, conductance, diag_inverse, cross_eff, transpose):
    current = apply_block(diag_inverse, cross_eff, rhs, transpose)
    for sweep_index in range(SWEEPS - 1):
        fluxes = conductance[:, None] * current
        along_y = with_halo(fluxes, (("sy", 3),), 1, True)
        along_x = with_halo(fluxes, (("sx", 2),), 1, False)
        source = rhs + conductance[:, None] * neighbour_parts(fluxes, along_x, along_y)
        current = apply_block(diag_inverse, cross_eff, source, transpose)
    return current


def local(
    directions,
    conductance,
    diag_inverse,
    cross_inverse,
    coupling,
    sensitivity,
    obs_weight,
    prior_weight,
):
    species_count, dir_count, size_x, size_y, size_z = directions.shape
    offdiag = coupling.astype(jnp.float32) * (1.0 - jnp.eye(species_count, dtype=jnp.float32))
    cross_eff = cross_inverse * offdiag[:, :, None, None, None]
    forward_rhs = sensitivity[:, None] * directions
    forward = jacobi_single(forward_rhs, conductance, diag_inverse, cross_eff, False)
    adjoint = jacobi_single(
        obs_weight[:, None] * forward, conductance, diag_inverse, cross_eff, True
    )
    hess_action = sensitivity[:, None] * adjoint + prior_weight[:, None] * directions
    regrouped = lax.all_to_all(hess_action, "dir", split_axis=4, concat_axis=1, tiled=True)
    total_rows = (
        species_count * size_x * size_y * size_z * lax.axis_size("sx") * lax.axis_size("sy")
    )
    gram_local = (
        jnp.einsum("sdxyz,sexyz->de", regrouped, regrouped, precision=lax.Precision.HIGHEST)
        / total_rows
    )
    gram_total = lax.psum(gram_local, ("sx", "sy", "dir"))
    r_factor = jnp.linalg.cholesky(gram_total).T
    return (hess_action, r_factor)


def solution(mesh):
    return jax.shard_map(
        local,
        mesh=mesh,
        in_specs=(
            P(None, "dir", "sx", "sy", None),
            P(None, "sx", "sy", None),
            P(None, "sx", "sy", None),
            P(None, None, "sx", "sy", None),
            P(),
            P(None, "sx", "sy", None),
            P(None, "sx", "sy", None),
            P(None, "sx", "sy", None),
        ),
        out_specs=(P(None, "dir", "sx", "sy", None), P()),
        check_vma=False,
    )
```

profile of v0, /device:TPU:1, one launch (start us, length us, event | category | flops | bytes accessed | tf_op | source)
XLA Modules:
  0.0 277.3 jit_solution(13699495258325066765)
XLA Ops:
  5.0 4.8 %collective-permute-start.3 = (f32[7,8,2,1,128]{4,1,3,2,0:T(8,128)S(1)}, f32[7,8,2,1,128]{4,1,3,2,0:T(8,128)S(1)}, u32[]{:S(2)}, u32[]{:S(2)}) collective-permute-start(f32[7,8,2,1,128]{4,1,3,2,0:T(8,128)S(1)} %copy.94), channel_id=1, source_target_pairs={{0,8},{8,16},{16,24},{24,32},{32,40},{40,48},{48,56},{56,0},{1,9},... | collective-permute-start | bytes 172040 | tf_op jit(solution)/shard_map/ppermute | solution.py:17
  9.8 8.7 %collective-permute-start.2 = (f32[7,8,2,1,128]{4,1,3,2,0:T(8,128)S(1)}, f32[7,8,2,1,128]{4,1,3,2,0:T(8,128)S(1)}, u32[]{:S(2)}, u32[]{:S(2)}) collective-permute-start(f32[7,8,2,1,128]{4,1,3,2,0:T(8,128)S(1)} %copy.92), channel_id=1, source_target_pairs={{8,0},{16,8},{24,16},{32,24},{40,32},{48,40},{56,48},{0,56},{9,1},... | collective-permute-start | bytes 172040 | tf_op jit(solution)/shard_map/ppermute | solution.py:19
  18.6 2.9 %collective-permute-start = (f32[7,8,1,8,128]{4,3,2,1,0:T(8,128)S(1)}, f32[7,8,1,8,128]{4,3,2,1,0:T(8,128)S(1)}, u32[]{:S(2)}, u32[]{:S(2)}) collective-permute-start(f32[7,8,1,8,128]{4,3,2,1,0:T(8,128)S(1)} %get-tuple-element.93), channel_id=1, source_target_pairs={{64,0},{128,64},{192,128},{256,192},{320,256},{384,320},{448,384},... | collective-permute-start | bytes 688136 | tf_op jit(solution)/shard_map/ppermute | solution.py:19
  21.5 3.0 %collective-permute-start.1 = (f32[7,8,1,8,128]{4,3,2,1,0:T(8,128)S(1)}, f32[7,8,1,8,128]{4,3,2,1,0:T(8,128)S(1)}, u32[]{:S(2)}, u32[]{:S(2)}) collective-permute-start(f32[7,8,1,8,128]{4,3,2,1,0:T(8,128)S(1)} %get-tuple-element.94), channel_id=1, source_target_pairs={{0,64},{64,128},{128,192},{192,256},{256,320},{320,384},{384,448},... | collective-permute-start | bytes 688136 | tf_op jit(solution)/shard_map/ppermute | solution.py:17
  28.4 1.9 collective-permute-start.7
  30.3 4.6 %collective-permute-start.6 = (f32[7,8,2,1,128]{4,1,3,2,0:T(8,128)S(1)}, f32[7,8,2,1,128]{4,1,3,2,0:T(8,128)S(1)}, u32[]{:S(2)}, u32[]{:S(2)}) collective-permute-start(f32[7,8,2,1,128]{4,1,3,2,0:T(8,128)S(1)} %copy.96), channel_id=1, source_target_pairs={{8,0},{16,8},{24,16},{32,24},{40,32},{48,40},{56,48},{0,56},{9,1},... | collective-permute-start | bytes 172040 | tf_op jit(solution)/shard_map/ppermute | solution.py:19
  36.8 4.9 %collective-permute-start.5 = (f32[7,8,1,8,128]{4,3,2,1,0:T(8,128)S(1)}, f32[7,8,1,8,128]{4,3,2,1,0:T(8,128)S(1)}, u32[]{:S(2)}, u32[]{:S(2)}) collective-permute-start(f32[7,8,1,8,128]{4,3,2,1,0:T(8,128)S(1)} %get-tuple-element.81), channel_id=1, source_target_pairs={{0,64},{64,128},{128,192},{192,256},{256,320},{320,384},{384,448},... | collective-permute-start | bytes 688136 | tf_op jit(solution)/shard_map/ppermute | solution.py:17
  47.5 4.6 %collective-permute-start.10 = (f32[7,8,2,1,128]{4,1,3,2,0:T(8,128)S(1)}, f32[7,8,2,1,128]{4,1,3,2,0:T(8,128)S(1)}, u32[]{:S(2)}, u32[]{:S(2)}) collective-permute-start(f32[7,8,2,1,128]{4,1,3,2,0:T(8,128)S(1)} %copy.100), channel_id=1, source_target_pairs={{8,0},{16,8},{24,16},{32,24},{40,32},{48,40},{56,48},{0,56},{9,1},... | collective-permute-start | bytes 172040 | tf_op jit(solution)/shard_map/ppermute | solution.py:19
  54.0 4.9 %collective-permute-start.9 = (f32[7,8,1,8,128]{4,3,2,1,0:T(8,128)S(1)}, f32[7,8,1,8,128]{4,3,2,1,0:T(8,128)S(1)}, u32[]{:S(2)}, u32[]{:S(2)}) collective-permute-start(f32[7,8,1,8,128]{4,3,2,1,0:T(8,128)S(1)} %get-tuple-element.68), channel_id=1, source_target_pairs={{0,64},{64,128},{128,192},{192,256},{256,320},{320,384},{384,448},... | collective-permute-start | bytes 688136 | tf_op jit(solution)/shard_map/ppermute | solution.py:17
  65.5 4.6 %collective-permute-start.14 = (f32[7,8,2,1,128]{4,1,3,2,0:T(8,128)S(1)}, f32[7,8,2,1,128]{4,1,3,2,0:T(8,128)S(1)}, u32[]{:S(2)}, u32[]{:S(2)}) collective-permute-start(f32[7,8,2,1,128]{4,1,3,2,0:T(8,128)S(1)} %copy.104), channel_id=1, source_target_pairs={{8,0},{16,8},{24,16},{32,24},{40,32},{48,40},{56,48},{0,56},{9,1},... | collective-permute-start | bytes 172040 | tf_op jit(solution)/shard_map/ppermute | solution.py:19
  72.0 4.9 %collective-permute-start.13 = (f32[7,8,1,8,128]{4,3,2,1,0:T(8,128)S(1)}, f32[7,8,1,8,128]{4,3,2,1,0:T(8,128)S(1)}, u32[]{:S(2)}, u32[]{:S(2)}) collective-permute-start(f32[7,8,1,8,128]{4,3,2,1,0:T(8,128)S(1)} %get-tuple-element.48), channel_id=1, source_target_pairs={{0,64},{64,128},{128,192},{192,256},{256,320},{320,384},{384,448},... | collective-permute-start | bytes 688136 | tf_op jit(solution)/shard_map/ppermute | solution.py:17
  83.0 4.6 %collective-permute-start.18 = (f32[7,8,2,1,128]{4,1,3,2,0:T(8,128)S(1)}, f32[7,8,2,1,128]{4,1,3,2,0:T(8,128)S(1)}, u32[]{:S(2)}, u32[]{:S(2)}) collective-permute-start(f32[7,8,2,1,128]{4,1,3,2,0:T(8,128)S(1)} %copy.108), channel_id=1, source_target_pairs={{8,0},{16,8},{24,16},{32,24},{40,32},{48,40},{56,48},{0,56},{9,1},... | collective-permute-start | bytes 172040 | tf_op jit(solution)/shard_map/ppermute | solution.py:19
  87.6 1.9 collective-permute-start.16
  89.5 4.9 %collective-permute-start.17 = (f32[7,8,1,8,128]{4,3,2,1,0:T(8,128)S(1)}, f32[7,8,1,8,128]{4,3,2,1,0:T(8,128)S(1)}, u32[]{:S(2)}, u32[]{:S(2)}) collective-permute-start(f32[7,8,1,8,128]{4,3,2,1,0:T(8,128)S(1)} %get-tuple-element.35), channel_id=1, source_target_pairs={{0,64},{64,128},{128,192},{192,256},{256,320},{320,384},{384,448},... | collective-permute-start | bytes 688136 | tf_op jit(solution)/shard_map/ppermute | solution.py:17
  100.6 4.6 %collective-permute-start.22 = (f32[7,8,2,1,128]{4,1,3,2,0:T(8,128)S(1)}, f32[7,8,2,1,128]{4,1,3,2,0:T(8,128)S(1)}, u32[]{:S(2)}, u32[]{:S(2)}) collective-permute-start(f32[7,8,2,1,128]{4,1,3,2,0:T(8,128)S(1)} %copy.112), channel_id=1, source_target_pairs={{8,0},{16,8},{24,16},{32,24},{40,32},{48,40},{56,48},{0,56},{9,1},... | collective-permute-start | bytes 172040 | tf_op jit(solution)/shard_map/ppermute | solution.py:19
  107.1 5.1 %collective-permute-start.21 = (f32[7,8,1,8,128]{4,3,2,1,0:T(8,128)S(1)}, f32[7,8,1,8,128]{4,3,2,1,0:T(8,128)S(1)}, u32[]{:S(2)}, u32[]{:S(2)}) collective-permute-start(f32[7,8,1,8,128]{4,3,2,1,0:T(8,128)S(1)} %get-tuple-element.22), channel_id=1, source_target_pairs={{0,64},{64,128},{128,192},{192,256},{256,320},{320,384},{384,448},... | collective-permute-start | bytes 688136 | tf_op jit(solution)/shard_map/ppermute | solution.py:17
  116.1 7.3 %copy.116 = f32[7,8,2,8,128]{3,1,2,0,4:T(8,128)} copy(f32[7,8,2,8,128]{4,3,2,1,0:T(8,128)S(1)} %multiply_add_fusion) | data formatting | bytes 917504 | tf_op jit(solution)/shard_map/add | solution.py:77
  123.4 6.0 %reshape.24 = f32[8,1,14336]{2,1,0:T(1,128)S(1)} reshape(f32[128,7,2,8,8]{4,3,2,1,0:T(8,128)} %bitcast.157) | data formatting | bytes 917504
  129.3 19.3 %all_to_all.18 = f32[8,1,14336]{2,1,0:T(1,128)S(1)} all-to-all(f32[8,1,14336]{2,1,0:T(1,128)S(1)} %reshape.24), channel_id=1, replica_groups=mesh['sx'=8,'sy'=8,'dir'=8] {'dir'}, dimensions={0} | all-to-all | bytes 917504 | tf_op jit(solution)/shard_map/all_to_all | solution.py:78
  150.9 7.1 %reshape.25 = f32[128,7,2,8,8]{4,3,2,1,0:T(8,128)} reshape(f32[8,14336]{1,0:T(8,128)S(1)} %reduce.6) | data formatting | bytes 917504
  158.0 6.6 %copy.117 = f32[7,8,2,8,8,16]{5,3,2,1,4,0:T(8,128)} copy(f32[7,8,2,8,8,16]{3,1,2,0,5,4:T(8,128)} %bitcast.156) | data formatting | bytes 917504 | tf_op jit(solution)/shard_map/all_to_all | solution.py:78
  164.6 8.4 %fusion.5 = f32[64,64]{0,1:T(8,128)S(1)} fusion(f32[7,64,2,8,16]{4,3,2,1,0:T(8,128)} %bitcast.158), kind=kOutput, calls=%fused_computation.3 | convolution fusion | flops 88084480 | bytes 475136 | tf_op jit(solution)/shard_map/sdxyz,sexyz->de/dot_general | solution.py:83
  173.0 96.3 %psum.7 = f32[64,64]{0,1:T(8,128)S(1)} all-reduce(f32[64,64]{0,1:T(8,128)S(1)} %fusion.5), channel_id=1, replica_groups=mesh['sx'=8,'sy'=8,'dir'=8] {'sx','sy','dir'}, use_global_device_ids=true, to_apply=%region_0.0 | all-reduce | flops 4096 | bytes 32768 | tf_op jit(solution)/shard_map/psum | solution.py:86
  269.4 5.8 %cholesky.18 = f32[64,64]{1,0:T(8,128)S(1)} custom-call(f32[64,64]{1,0:T(8,128)S(1)} %fusion.50), custom_call_target="Cholesky" | custom-call | tf_op jit(solution)/shard_map/jit(cholesky)/cholesky | solution.py:87
  (123 shorter events, 48.0 us)
Async XLA Ops:
  5.0 19.8 %collective-permute-start.3 = (f32[7,8,2,1,128]{4,1,3,2,0:T(8,128)S(1)}, f32[7,8,2,1,128]{4,1,3,2,0:T(8,128)S(1)}, u32[]{:S(2)}, u32[]{:S(2)}) collective-permute-start(f32[7,8,2,1,128]{4,1,3,2,0:T(8,128)S(1)} %copy.94), channel_id=1, source_target_pairs={{0,8},{8,16},{16,24},{24,32},{32,40},{40,48},{48,56},{56,0},{1,9},... | collective-permute-start | bytes 172040 | tf_op jit(solution)/shard_map/ppermute | solution.py:17
  9.8 15.0 %collective-permute-start.2 = (f32[7,8,2,1,128]{4,1,3,2,0:T(8,128)S(1)}, f32[7,8,2,1,128]{4,1,3,2,0:T(8,128)S(1)}, u32[]{:S(2)}, u32[]{:S(2)}) collective-permute-start(f32[7,8,2,1,128]{4,1,3,2,0:T(8,128)S(1)} %copy.92), channel_id=1, source_target_pairs={{8,0},{16,8},{24,16},{32,24},{40,32},{48,40},{56,48},{0,56},{9,1},... | collective-permute-start | bytes 172040 | tf_op jit(solution)/shard_map/ppermute | solution.py:19
  18.6 7.7 %collective-permute-start = (f32[7,8,1,8,128]{4,3,2,1,0:T(8,128)S(1)}, f32[7,8,1,8,128]{4,3,2,1,0:T(8,128)S(1)}, u32[]{:S(2)}, u32[]{:S(2)}) collective-permute-start(f32[7,8,1,8,128]{4,3,2,1,0:T(8,128)S(1)} %get-tuple-element.93), channel_id=1, source_target_pairs={{64,0},{128,64},{192,128},{256,192},{320,256},{384,320},{448,384},... | collective-permute-start | bytes 688136 | tf_op jit(solution)/shard_map/ppermute | solution.py:19
  21.5 6.0 %collective-permute-start.1 = (f32[7,8,1,8,128]{4,3,2,1,0:T(8,128)S(1)}, f32[7,8,1,8,128]{4,3,2,1,0:T(8,128)S(1)}, u32[]{:S(2)}, u32[]{:S(2)}) collective-permute-start(f32[7,8,1,8,128]{4,3,2,1,0:T(8,128)S(1)} %get-tuple-element.94), channel_id=1, source_target_pairs={{0,64},{64,128},{128,192},{192,256},{256,320},{320,384},{384,448},... | collective-permute-start | bytes 688136 | tf_op jit(solution)/shard_map/ppermute | solution.py:17
  28.4 13.6 %collective-permute-start.7 = (f32[7,8,2,1,128]{4,1,3,2,0:T(8,128)S(1)}, f32[7,8,2,1,128]{4,1,3,2,0:T(8,128)S(1)}, u32[]{:S(2)}, u32[]{:S(2)}) collective-permute-start(f32[7,8,2,1,128]{4,1,3,2,0:T(8,128)S(1)} %copy.98), channel_id=1, source_target_pairs={{0,8},{8,16},{16,24},{24,32},{32,40},{40,48},{48,56},{56,0},{1,9},... | collective-permute-start | bytes 172040 | tf_op jit(solution)/shard_map/ppermute | solution.py:17
  30.3 11.7 %collective-permute-start.6 = (f32[7,8,2,1,128]{4,1,3,2,0:T(8,128)S(1)}, f32[7,8,2,1,128]{4,1,3,2,0:T(8,128)S(1)}, u32[]{:S(2)}, u32[]{:S(2)}) collective-permute-start(f32[7,8,2,1,128]{4,1,3,2,0:T(8,128)S(1)} %copy.96), channel_id=1, source_target_pairs={{8,0},{16,8},{24,16},{32,24},{40,32},{48,40},{56,48},{0,56},{9,1},... | collective-permute-start | bytes 172040 | tf_op jit(solution)/shard_map/ppermute | solution.py:19
  34.9 8.6 %collective-permute-start.4 = (f32[7,8,1,8,128]{4,3,2,1,0:T(8,128)S(1)}, f32[7,8,1,8,128]{4,3,2,1,0:T(8,128)S(1)}, u32[]{:S(2)}, u32[]{:S(2)}) collective-permute-start(f32[7,8,1,8,128]{4,3,2,1,0:T(8,128)S(1)} %get-tuple-element.80), channel_id=1, source_target_pairs={{64,0},{128,64},{192,128},{256,192},{320,256},{384,320},{448,384},... | collective-permute-start | bytes 688136 | tf_op jit(solution)/shard_map/ppermute | solution.py:19
  36.8 7.9 %collective-permute-start.5 = (f32[7,8,1,8,128]{4,3,2,1,0:T(8,128)S(1)}, f32[7,8,1,8,128]{4,3,2,1,0:T(8,128)S(1)}, u32[]{:S(2)}, u32[]{:S(2)}) collective-permute-start(f32[7,8,1,8,128]{4,3,2,1,0:T(8,128)S(1)} %get-tuple-element.81), channel_id=1, source_target_pairs={{0,64},{64,128},{128,192},{192,256},{256,320},{320,384},{384,448},... | collective-permute-start | bytes 688136 | tf_op jit(solution)/shard_map/ppermute | solution.py:17
  45.6 13.6 %collective-permute-start.11 = (f32[7,8,2,1,128]{4,1,3,2,0:T(8,128)S(1)}, f32[7,8,2,1,128]{4,1,3,2,0:T(8,128)S(1)}, u32[]{:S(2)}, u32[]{:S(2)}) collective-permute-start(f32[7,8,2,1,128]{4,1,3,2,0:T(8,128)S(1)} %copy.102), channel_id=1, source_target_pairs={{0,8},{8,16},{16,24},{24,32},{32,40},{40,48},{48,56},{56,0},{1,9},... | collective-permute-start | bytes 172040 | tf_op jit(solution)/shard_map/ppermute | solution.py:17
  47.5 11.7 %collective-permute-start.10 = (f32[7,8,2,1,128]{4,1,3,2,0:T(8,128)S(1)}, f32[7,8,2,1,128]{4,1,3,2,0:T(8,128)S(1)}, u32[]{:S(2)}, u32[]{:S(2)}) collective-permute-start(f32[7,8,2,1,128]{4,1,3,2,0:T(8,128)S(1)} %copy.100), channel_id=1, source_target_pairs={{8,0},{16,8},{24,16},{32,24},{40,32},{48,40},{56,48},{0,56},{9,1},... | collective-permute-start | bytes 172040 | tf_op jit(solution)/shard_map/ppermute | solution.py:19
  52.1 8.6 %collective-permute-start.8 = (f32[7,8,1,8,128]{4,3,2,1,0:T(8,128)S(1)}, f32[7,8,1,8,128]{4,3,2,1,0:T(8,128)S(1)}, u32[]{:S(2)}, u32[]{:S(2)}) collective-permute-start(f32[7,8,1,8,128]{4,3,2,1,0:T(8,128)S(1)} %get-tuple-element.67), channel_id=1, source_target_pairs={{64,0},{128,64},{192,128},{256,192},{320,256},{384,320},{448,384},... | collective-permute-start | bytes 688136 | tf_op jit(solution)/shard_map/ppermute | solution.py:19
  54.0 7.9 %collective-permute-start.9 = (f32[7,8,1,8,128]{4,3,2,1,0:T(8,128)S(1)}, f32[7,8,1,8,128]{4,3,2,1,0:T(8,128)S(1)}, u32[]{:S(2)}, u32[]{:S(2)}) collective-permute-start(f32[7,8,1,8,128]{4,3,2,1,0:T(8,128)S(1)} %get-tuple-element.68), channel_id=1, source_target_pairs={{0,64},{64,128},{128,192},{192,256},{256,320},{320,384},{384,448},... | collective-permute-start | bytes 688136 | tf_op jit(solution)/shard_map/ppermute | solution.py:17
  63.6 13.6 %collective-permute-start.15 = (f32[7,8,2,1,128]{4,1,3,2,0:T(8,128)S(1)}, f32[7,8,2,1,128]{4,1,3,2,0:T(8,128)S(1)}, u32[]{:S(2)}, u32[]{:S(2)}) collective-permute-start(f32[7,8,2,1,128]{4,1,3,2,0:T(8,128)S(1)} %copy.106), channel_id=1, source_target_pairs={{0,8},{8,16},{16,24},{24,32},{32,40},{40,48},{48,56},{56,0},{1,9},... | collective-permute-start | bytes 172040 | tf_op jit(solution)/shard_map/ppermute | solution.py:17
  65.5 11.7 %collective-permute-start.14 = (f32[7,8,2,1,128]{4,1,3,2,0:T(8,128)S(1)}, f32[7,8,2,1,128]{4,1,3,2,0:T(8,128)S(1)}, u32[]{:S(2)}, u32[]{:S(2)}) collective-permute-start(f32[7,8,2,1,128]{4,1,3,2,0:T(8,128)S(1)} %copy.104), channel_id=1, source_target_pairs={{8,0},{16,8},{24,16},{32,24},{40,32},{48,40},{56,48},{0,56},{9,1},... | collective-permute-start | bytes 172040 | tf_op jit(solution)/shard_map/ppermute | solution.py:19
  70.1 8.6 %collective-permute-start.12 = (f32[7,8,1,8,128]{4,3,2,1,0:T(8,128)S(1)}, f32[7,8,1,8,128]{4,3,2,1,0:T(8,128)S(1)}, u32[]{:S(2)}, u32[]{:S(2)}) collective-permute-start(f32[7,8,1,8,128]{4,3,2,1,0:T(8,128)S(1)} %get-tuple-element.47), channel_id=1, source_target_pairs={{64,0},{128,64},{192,128},{256,192},{320,256},{384,320},{448,384},... | collective-permute-start | bytes 688136 | tf_op jit(solution)/shard_map/ppermute | solution.py:19
  72.0 7.9 %collective-permute-start.13 = (f32[7,8,1,8,128]{4,3,2,1,0:T(8,128)S(1)}, f32[7,8,1,8,128]{4,3,2,1,0:T(8,128)S(1)}, u32[]{:S(2)}, u32[]{:S(2)}) collective-permute-start(f32[7,8,1,8,128]{4,3,2,1,0:T(8,128)S(1)} %get-tuple-element.48), channel_id=1, source_target_pairs={{0,64},{64,128},{128,192},{192,256},{256,320},{320,384},{384,448},... | collective-permute-start | bytes 688136 | tf_op jit(solution)/shard_map/ppermute | solution.py:17
  81.1 13.6 %collective-permute-start.19 = (f32[7,8,2,1,128]{4,1,3,2,0:T(8,128)S(1)}, f32[7,8,2,1,128]{4,1,3,2,0:T(8,128)S(1)}, u32[]{:S(2)}, u32[]{:S(2)}) collective-permute-start(f32[7,8,2,1,128]{4,1,3,2,0:T(8,128)S(1)} %copy.110), channel_id=1, source_target_pairs={{0,8},{8,16},{16,24},{24,32},{32,40},{40,48},{48,56},{56,0},{1,9},... | collective-permute-start | bytes 172040 | tf_op jit(solution)/shard_map/ppermute | solution.py:17
  83.0 11.7 %collective-permute-start.18 = (f32[7,8,2,1,128]{4,1,3,2,0:T(8,128)S(1)}, f32[7,8,2,1,128]{4,1,3,2,0:T(8,128)S(1)}, u32[]{:S(2)}, u32[]{:S(2)}) collective-permute-start(f32[7,8,2,1,128]{4,1,3,2,0:T(8,128)S(1)} %copy.108), channel_id=1, source_target_pairs={{8,0},{16,8},{24,16},{32,24},{40,32},{48,40},{56,48},{0,56},{9,1},... | collective-permute-start | bytes 172040 | tf_op jit(solution)/shard_map/ppermute | solution.py:19
  87.6 8.6 %collective-permute-start.16 = (f32[7,8,1,8,128]{4,3,2,1,0:T(8,128)S(1)}, f32[7,8,1,8,128]{4,3,2,1,0:T(8,128)S(1)}, u32[]{:S(2)}, u32[]{:S(2)}) collective-permute-start(f32[7,8,1,8,128]{4,3,2,1,0:T(8,128)S(1)} %get-tuple-element.34), channel_id=1, source_target_pairs={{64,0},{128,64},{192,128},{256,192},{320,256},{384,320},{448,384},... | collective-permute-start | bytes 688136 | tf_op jit(solution)/shard_map/ppermute | solution.py:19
  89.5 7.9 %collective-permute-start.17 = (f32[7,8,1,8,128]{4,3,2,1,0:T(8,128)S(1)}, f32[7,8,1,8,128]{4,3,2,1,0:T(8,128)S(1)}, u32[]{:S(2)}, u32[]{:S(2)}) collective-permute-start(f32[7,8,1,8,128]{4,3,2,1,0:T(8,128)S(1)} %get-tuple-element.35), channel_id=1, source_target_pairs={{0,64},{64,128},{128,192},{192,256},{256,320},{320,384},{384,448},... | collective-permute-start | bytes 688136 | tf_op jit(solution)/shard_map/ppermute | solution.py:17
  98.6 13.8 %collective-permute-start.23 = (f32[7,8,2,1,128]{4,1,3,2,0:T(8,128)S(1)}, f32[7,8,2,1,128]{4,1,3,2,0:T(8,128)S(1)}, u32[]{:S(2)}, u32[]{:S(2)}) collective-permute-start(f32[7,8,2,1,128]{4,1,3,2,0:T(8,128)S(1)} %copy.114), channel_id=1, source_target_pairs={{0,8},{8,16},{16,24},{24,32},{32,40},{40,48},{48,56},{56,0},{1,9},... | collective-permute-start | bytes 172040 | tf_op jit(solution)/shard_map/ppermute | solution.py:17
  100.6 11.9 %collective-permute-start.22 = (f32[7,8,2,1,128]{4,1,3,2,0:T(8,128)S(1)}, f32[7,8,2,1,128]{4,1,3,2,0:T(8,128)S(1)}, u32[]{:S(2)}, u32[]{:S(2)}) collective-permute-start(f32[7,8,2,1,128]{4,1,3,2,0:T(8,128)S(1)} %copy.112), channel_id=1, source_target_pairs={{8,0},{16,8},{24,16},{32,24},{40,32},{48,40},{56,48},{0,56},{9,1},... | collective-permute-start | bytes 172040 | tf_op jit(solution)/shard_map/ppermute | solution.py:19
  105.2 8.6 %collective-permute-start.20 = (f32[7,8,1,8,128]{4,3,2,1,0:T(8,128)S(1)}, f32[7,8,1,8,128]{4,3,2,1,0:T(8,128)S(1)}, u32[]{:S(2)}, u32[]{:S(2)}) collective-permute-start(f32[7,8,1,8,128]{4,3,2,1,0:T(8,128)S(1)} %get-tuple-element.21), channel_id=1, source_target_pairs={{64,0},{128,64},{192,128},{256,192},{320,256},{384,320},{448,384},... | collective-permute-start | bytes 688136 | tf_op jit(solution)/shard_map/ppermute | solution.py:19
  107.1 7.9 %collective-permute-start.21 = (f32[7,8,1,8,128]{4,3,2,1,0:T(8,128)S(1)}, f32[7,8,1,8,128]{4,3,2,1,0:T(8,128)S(1)}, u32[]{:S(2)}, u32[]{:S(2)}) collective-permute-start(f32[7,8,1,8,128]{4,3,2,1,0:T(8,128)S(1)} %get-tuple-element.22), channel_id=1, source_target_pairs={{0,64},{64,128},{128,192},{192,256},{256,320},{320,384},{384,448},... | collective-permute-start | bytes 688136 | tf_op jit(solution)/shard_map/ppermute | solution.py:17
  (7 other events, 110.1 us)
where the time goes:
time: 278 us; the launch traced here: 277 us
  blocking collectives  116 us (42%)
  starting transfers between devices  86.4 us (31%)
  local copies, waits for them, and re-layouts  31.1 us (11%)
  other arithmetic  18.8 us (7%)
  waiting for transfers between devices  15.4 us (6%)
  matrix products  8.41 us (3%)
    psum x1, blocking collectives, local(): gram_total = lax.psum(gram_local, ('sx', 'sy', 'dir'))  96.3 us
    ppermute x12, starting transfers between devices, with_halo(): lax.ppermute(head, axis, [((i + 1) % count, i) for i in range(ends)])  44 us
    ppermute x12, starting transfers between devices, with_halo(): lax.ppermute(tail, axis, [(i, (i + 1) % count) for i in range(ends)])  42.4 us
    all_to_all x1, blocking collectives, local(): lax.all_to_all(hess_action, 'dir', split_axis=4, concat_axis=1, tiled=True)  19.3 us
    unnamed x17, local copies, waits for them, and re-layouts  13.8 us
    dot_general x1, matrix products, local(): jnp.einsum('sdxyz,sexyz->de', regrouped, regrouped, precision=lax.Precisi...  8.41 us
    ppermute x12, waiting for transfers between devices, with_halo(): lax.ppermute(head, axis, [((i + 1) % count, i) for i in range(ends)])  8.29 us
    add x1, local copies, waits for them, and re-layouts, local(): sensitivity[:, None] * adjoint + prior_weight[:, None] * directions  7.25 us
  transfers between devices with their start and end apart: 24, of which 12 were waited for; matrix products, arithmetic and copies ran while one was open for 1% of the time, Pallas kernels for 0%

commit v1 on v0

v1 whole, which is shorter than its diff:
```python
import functools

import jax
import jax.numpy as jnp
from jax import lax
from jax.experimental import pallas as pl
from jax.experimental.pallas import tpu as pltpu
from jax.sharding import PartitionSpec as P

SPEC = 7
KDEV = 8
LX = 2
LY = 8
NZ = 128
PAIRS = SPEC * LX
F32 = jnp.float32


def row(ref, index):
    return jnp.broadcast_to(ref[pl.ds(index, 1), :], (KDEV, NZ))


def block_terms(beff, source, cell, transpose):
    out = []
    for s in range(SPEC):
        total = row(beff, (s * SPEC + s) * LX * LY + cell) * source[s]
        for t in range(SPEC):
            if t != s:
                entry = t * SPEC + s if transpose else s * SPEC + t
                total = total + row(beff, entry * LX * LY + cell) * source[t]
        out.append(total)
    return out


def parities():
    return lax.rem(lax.axis_index("sx"), 2), lax.rem(lax.axis_index("sy"), 2)


def store_sends(flux, cross, inside, ya, yb):
    px, py = parities()
    cross[...] = flux[:, px]
    inside[...] = flux[:, 1 - px]
    ya[...] = flux[:, :, 7 * (1 - py)]
    yb[...] = flux[:, :, 7 * py]


def first_kernel(dirs, cond, diag, crossinv, coup, sens, beff, rhs, flux, cross, inside, ya, yb):
    for s in range(SPEC):
        for t in range(SPEC):
            here = pl.ds((s * SPEC + t) * LX * LY, LX * LY)
            if s == t:
                beff[here, :] = diag[pl.ds(s * LX * LY, LX * LY), :]
            else:
                beff[here, :] = crossinv[here, :] * coup[s, t].astype(F32)

    def body(y, carry):
        for x in range(LX):
            cell = x * LY + y
            source = []
            for s in range(SPEC):
                d = dirs[pl.ds(s * KDEV * LX * LY + cell, KDEV, stride=LX * LY), :]
                r = row(sens, s * LX * LY + cell) * d
                rhs[s, x, y] = r
                source.append(r)
            values = block_terms(beff, source, cell, False)
            for s in range(SPEC):
                flux[s, x, y] = row(cond, s * LX * LY + cell) * values[s]
        return carry

    lax.fori_loop(0, LY, body, 0)
    store_sends(flux, cross, inside, ya, yb)


def fill_wide(wide, flux, rcross, rinside, rya, ryb):
    px, py = parities()
    wide[:, 1:3, 1:9] = flux[...]
    wide[:, 3 * px, 1:9] = rcross[...]
    wide[:, 3 * (1 - px), 1:9] = rinside[...]
    wide[:, 1:3, 9 * (1 - py)] = rya[...]
    wide[:, 1:3, 9 * py] = ryb[...]


def source_terms(wide, rhs, cond, x, y, cell, lane):
    source = []
    for s in range(SPEC):
        centre = wide[s, x + 1, y + 1]
        total = wide[s, x + 2, y + 1] + wide[s, x, y + 1]
        total = total + wide[s, x + 1, y + 2]
        total = total + wide[s, x + 1, y]
        total = total + jnp.where(lane == NZ - 1, 0.0, pltpu.roll(centre, NZ - 1, 1))
        total = total + jnp.where(lane == 0, 0.0, pltpu.roll(centre, 1, 1))
        source.append(rhs[s, x, y] + row(cond, s * LX * LY + cell) * total)
    return source


def sweep_kernel(transpose, fluxin, rcross, rinside, rya, ryb, rhs, beff, cond,
                 flux, cross, inside, ya, yb, wide):
    fill_wide(wide, fluxin, rcross, rinside, rya, ryb)
    lane = lax.broadcasted_iota(jnp.int32, (KDEV, NZ), 1)

    def body(y, carry):
        for x in range(LX):
            cell = x * LY + y
            source = source_terms(wide, rhs, cond, x, y, cell, lane)
            values = block_terms(beff, source, cell, transpose)
            for s in range(SPEC):
                flux[s, x, y] = row(cond, s * LX * LY + cell) * values[s]
        return carry

    lax.fori_loop(0, LY, body, 0)
    store_sends(flux, cross, inside, ya, yb)


def turn_kernel(fluxin, rcross, rinside, rya, ryb, rhs, beff, cond, obs,
                rhs2, flux, cross, inside, ya, yb, wide):
    fill_wide(wide, fluxin, rcross, rinside, rya, ryb)
    lane = lax.broadcasted_iota(jnp.int32, (KDEV, NZ), 1)

    def body(y, carry):
        for x in range(LX):
            cell = x * LY + y
            source = source_terms(wide, rhs, cond, x, y, cell, lane)
            forward = block_terms(beff, source, cell, False)
            second = []
            for s in range(SPEC):
                r = row(obs, s * LX * LY + cell) * forward[s]
                rhs2[s, x, y] = r
                second.append(r)
            values = block_terms(beff, second, cell, True)
            for s in range(SPEC):
                flux[s, x, y] = row(cond, s * LX * LY + cell) * values[s]
        return carry

    lax.fori_loop(0, LY, body, 0)
    store_sends(flux, cross, inside, ya, yb)


def last_kernel(fluxin, rcross, rinside, rya, ryb, rhs, beff, cond, sens, prior, dirs,
                hess, spread, wide):
    fill_wide(wide, fluxin, rcross, rinside, rya, ryb)
    lane = lax.broadcasted_iota(jnp.int32, (KDEV, NZ), 1)

    def body(y, carry):
        for x in range(LX):
            cell = x * LY + y
            source = source_terms(wide, rhs, cond, x, y, cell, lane)
            values = block_terms(beff, source, cell, True)
            for s in range(SPEC):
                rows = pl.ds(s * KDEV * LX * LY + cell, KDEV, stride=LX * LY)
                h = row(sens, s * LX * LY + cell) * values[s]
                h = h + row(prior, s * LX * LY + cell) * dirs[rows, :]
                hess[rows, :] = h
                spread[y, :, pl.ds((s * LX + x) * NZ, NZ)] = h
        return carry

    lax.fori_loop(0, LY, body, 0)


def gram_kernel(scale, actions, out):
    a = actions[...]
    gram = lax.dot_general(
        a, a, (((1,), (1,)), ((), ())),
        precision=lax.Precision.HIGHEST, preferred_element_type=F32,
    ) * scale
    packed = jnp.concatenate([gram[:32], gram[32:]], axis=1)
    for k in range(8):
        out[k] = packed


def reduce_kernel(parts, out):
    total = parts[0]
    for k in range(1, 8):
        total = total + parts[k]
    for k in range(8):
        out[k] = total


def unpack_kernel(parts, out):
    total = parts[0]
    for k in range(1, 8):
        total = total + parts[k]
    out[...] = jnp.concatenate([total[:, :64], total[:, 64:]], axis=0)


def call(body, out_shapes, smem=(), scratch=(), flops=1000, name=None):
    def run(*args):
        vmem = pl.BlockSpec(memory_space=pltpu.VMEM)
        specs = [
            pl.BlockSpec(memory_space=pltpu.SMEM) if i in smem else vmem
            for i in range(len(args))
        ]
        return pl.pallas_call(
            body,
            out_shape=[jax.ShapeDtypeStruct(s, F32) for s in out_shapes],
            in_specs=specs,
            out_specs=[vmem] * len(out_shapes),
            scratch_shapes=list(scratch),
            compiler_params=pltpu.CompilerParams(vmem_limit_bytes=12 << 20),
            name=name,
        )(*args)

    return run


STATE = (SPEC, LX, LY, KDEV, NZ)
SENDS = [(SPEC, LY, KDEV, NZ)] * 2 + [(SPEC, LX, KDEV, NZ)] * 2
WIDE = pltpu.VMEM((SPEC, LX + 2, LY + 2, KDEV, NZ), F32)


def exchange(cross, inside, ya, yb):
    nx, ny = lax.axis_size("sx"), lax.axis_size("sy")
    inner = [(i, i ^ 1) for i in range(nx)]
    outer = [(i, i + 1 if i % 2 else i - 1) for i in range(1, nx - 1)]
    even = [(i, i ^ 1) for i in range(ny)]
    odd = [(i, (i + 1) % ny if i % 2 else (i - 1) % ny) for i in range(ny)]
    return (
        lax.ppermute(cross, "sx", outer),
        lax.ppermute(inside, "sx", inner),
        lax.ppermute(ya, "sy", even),
        lax.ppermute(yb, "sy", odd),
    )


def local(dirs, cond, diag, crossinv, coup, sens, obs, prior):
    flat = lambda a: a.reshape(-1, NZ)
    hess_shape = dirs.shape
    dirs, cond, diag, crossinv, sens, obs, prior = map(
        flat, (dirs, cond, diag, crossinv, sens, obs, prior)
    )
    beff, rhs, flux, *sends = call(
        first_kernel, [(SPEC * SPEC * LX * LY, NZ), STATE, STATE] + SENDS, smem=(4,), name="first"
    )(dirs, cond, diag, crossinv, coup, sens)
    sweep = lambda transpose: call(
        functools.partial(sweep_kernel, transpose), [STATE] + SENDS, scratch=[WIDE], name="sweep"
    )
    for _ in range(2):
        flux, *sends = sweep(False)(flux, *exchange(*sends), rhs, beff, cond)
    rhs, flux, *sends = call(turn_kernel, [STATE, STATE] + SENDS, scratch=[WIDE], name="turn")(
        flux, *exchange(*sends), rhs, beff, cond, obs
    )
    for _ in range(2):
        flux, *sends = sweep(True)(flux, *exchange(*sends), rhs, beff, cond)
    hess, spread = call(
        last_kernel, [dirs.shape, (LY, KDEV, PAIRS * NZ)], scratch=[WIDE], name="last"
    )(flux, *exchange(*sends), rhs, beff, cond, sens, prior, dirs)

    gathered = lax.all_to_all(spread, "dir", split_axis=0, concat_axis=0, tiled=True)
    gathered = gathered.reshape(8 * KDEV, PAIRS * NZ)
    rows = SPEC * LX * LY * NZ * lax.axis_size("sx") * lax.axis_size("sy")
    (parts,) = call(functools.partial(gram_kernel, 1.0 / rows), [(8, 32, 128)], name="gram")(gathered)
    parts = lax.all_to_all(parts, "sx", split_axis=0, concat_axis=0, tiled=True)
    (parts,) = call(reduce_kernel, [(8, 32, 128)], name="reduce_sx")(parts)
    parts = lax.all_to_all(parts, "sy", split_axis=0, concat_axis=0, tiled=True)
    (parts,) = call(reduce_kernel, [(8, 32, 128)], name="reduce_sy")(parts)
    parts = lax.all_to_all(parts, "dir", split_axis=0, concat_axis=0, tiled=True)
    (gram,) = call(unpack_kernel, [(64, 64)], name="unpack")(parts)
    r_factor = jnp.linalg.cholesky(gram).T
    return hess.reshape(hess_shape), r_factor


def solution(mesh):
    cells = P(None, "sx", "sy", None)
    return jax.shard_map(
        local,
        mesh=mesh,
        in_specs=(
            P(None, "dir", "sx", "sy", None), cells, cells,
            P(None, None, "sx", "sy", None), P(), cells, cells, cells,
        ),
        out_specs=(P(None, "dir", "sx", "sy", None), P()),
        check_vma=False,
    )
```

time: 278 us -> 172 us (0.62)
  blocking collectives: 116 us -> 54.2 us
  local copies, waits for them, and re-layouts: 31.1 us -> 5.94 us
  other arithmetic: 18.8 us -> 7.18 us
  Pallas kernels: 0 us -> 10 us
  matrix products: 8.41 us -> 0 us
  waiting for transfers between devices: 15.4 us -> 9.3 us
  starting transfers between devices: 86.4 us -> 82.2 us
    psum x1 -> x0, blocking collectives: 96.3 us -> none  [local(): gram_total = lax.psum(gram_local, ('sx', 'sy', 'dir'))]
    all_to_all x1 -> x4, blocking collectives: 19.3 us -> 54.2 us  [the longest x1 19.7 us: local(): lax.all_to_all(spread, 'dir', split_axis=0, concat_axis=0, tiled=True)]
    pallas_call x0 -> x11, Pallas kernels: none -> 10 us  [run(): pl.pallas_call(body, out_shape=[jax.ShapeDtypeStruct(s, F32) for s in out...]
    dot_general x1 -> x0, matrix products: 8.41 us -> none  [local(): jnp.einsum('sdxyz,sexyz->de', regrouped, regrouped, precision=lax.Precisi...]
    unnamed x17 -> x19, local copies, waits for them, and re-layouts: 13.8 us -> 5.86 us
    add x1 -> x0, local copies, waits for them, and re-layouts: 7.25 us -> none  [local(): sensitivity[:, None] * adjoint + prior_weight[:, None] * directions]
    all_to_all x2 -> x0, local copies, waits for them, and re-layouts: 7.08 us -> none  [local(): lax.all_to_all(hess_action, 'dir', split_axis=4, concat_axis=1, tiled=True)]
    mul x10 -> x0, other arithmetic: 6.38 us -> none  [the longest x6 3.15 us: jacobi_single(): fluxes = conductance[:, None] * current]
  transfers between devices with their start and end apart: 24 -> 24, of which waited for: 12 -> 6; matrix products, arithmetic and copies ran while one was open for 1% -> 0% of each run, Pallas kernels for 0% -> 0%
where the time goes in v1:
time: 172 us; the launch traced here: 170 us
  starting transfers between devices  82.2 us (48%)
  blocking collectives  54.2 us (32%)
  Pallas kernels  10 us (6%)
  waiting for transfers between devices  9.3 us (5%)
  other arithmetic  7.18 us (4%)
  local copies, waits for them, and re-layouts  5.94 us (3%)
    ppermute x6, starting transfers between devices, exchange(): lax.ppermute(yb, 'sy', odd)  31.5 us
    ppermute x6, starting transfers between devices, exchange(): lax.ppermute(cross, 'sx', outer)  24.2 us
    all_to_all x1, blocking collectives, local(): lax.all_to_all(spread, 'dir', split_axis=0, concat_axis=0, tiled=True)  19.7 us
    ppermute x6, starting transfers between devices, exchange(): lax.ppermute(inside, 'sx', inner)  14.5 us
    all_to_all x1, blocking collectives, local(): parts = lax.all_to_all(parts, 'sy', split_axis=0, concat_axis=0, tiled=True)  12.5 us
    ppermute x6, starting transfers between devices, exchange(): lax.ppermute(ya, 'sy', even)  12 us
    all_to_all x1, blocking collectives, local(): parts = lax.all_to_all(parts, 'sx', split_axis=0, concat_axis=0, tiled=True)  11.6 us
    all_to_all x1, blocking collectives, local(): lax.all_to_all(parts, 'dir', split_axis=0, concat_axis=0, tiled=True)  10.4 us
  transfers between devices with their start and end apart: 24, of which 6 were waited for; matrix products, arithmetic and copies ran while one was open for 0% of the time, Pallas kernels for 0%

profile of v1, /device:TPU:1, one launch (start us, length us, event | category | flops | bytes accessed | tf_op | source)
XLA Modules:
  0.0 169.8 jit_solution(1343470174258073090)
XLA Ops:
  7.1 4.5 %collective-permute-start = (f32[7,8,8,128]{3,2,1,0:T(8,128)S(1)}, f32[7,8,8,128]{3,2,1,0:T(8,128)S(1)}, u32[]{:S(2)}, u32[]{:S(2)}) collective-permute-start(f32[7,8,8,128]{3,2,1,0:T(8,128)S(1)} %get-tuple-element.38), channel_id=1, source_target_pairs={{64,128},{128,64},{192,256},{256,192},{320,384},{384,320},{65,129}... | collective-permute-start | bytes 688136 | tf_op jit(solution)/shard_map/ppermute | solution.py:217
  11.6 4.9 %collective-permute-start.1 = (f32[7,8,8,128]{3,2,1,0:T(8,128)S(1)}, f32[7,8,8,128]{3,2,1,0:T(8,128)S(1)}, u32[]{:S(2)}, u32[]{:S(2)}) collective-permute-start(f32[7,8,8,128]{3,2,1,0:T(8,128)S(1)} %get-tuple-element.39), channel_id=1, source_target_pairs={{0,64},{64,0},{128,192},{192,128},{256,320},{320,256},{384,448},{4... | collective-permute-start | bytes 688136 | tf_op jit(solution)/shard_map/ppermute | solution.py:218
  18.5 7.9 %collective-permute-start.3 = (f32[7,2,8,128]{3,2,1,0:T(8,128)S(1)}, f32[7,2,8,128]{3,2,1,0:T(8,128)S(1)}, u32[]{:S(2)}, u32[]{:S(2)}) collective-permute-start(f32[7,2,8,128]{3,2,1,0:T(8,128)S(1)} %get-tuple-element.41), channel_id=1, source_target_pairs={{0,56},{8,16},{16,8},{24,32},{32,24},{40,48},{48,40},{56,0},{1,57}... | collective-permute-start | bytes 172040 | tf_op jit(solution)/shard_map/ppermute | solution.py:220
  29.1 4.7 %collective-permute-start.4 = (f32[7,8,8,128]{3,2,1,0:T(8,128)S(1)}, f32[7,8,8,128]{3,2,1,0:T(8,128)S(1)}, u32[]{:S(2)}, u32[]{:S(2)}) collective-permute-start(f32[7,8,8,128]{3,2,1,0:T(8,128)S(1)} %get-tuple-element.45), channel_id=1, source_target_pairs={{64,128},{128,64},{192,256},{256,192},{320,384},{384,320},{65,129}... | collective-permute-start | bytes 688136 | tf_op jit(solution)/shard_map/ppermute | solution.py:217
  37.6 4.9 %collective-permute-start.7 = (f32[7,2,8,128]{3,2,1,0:T(8,128)S(1)}, f32[7,2,8,128]{3,2,1,0:T(8,128)S(1)}, u32[]{:S(2)}, u32[]{:S(2)}) collective-permute-start(f32[7,2,8,128]{3,2,1,0:T(8,128)S(1)} %get-tuple-element.48), channel_id=1, source_target_pairs={{0,56},{8,16},{16,8},{24,32},{32,24},{40,48},{48,40},{56,0},{1,57}... | collective-permute-start | bytes 172040 | tf_op jit(solution)/shard_map/ppermute | solution.py:220
  45.2 4.3 %collective-permute-start.8 = (f32[7,8,8,128]{3,2,1,0:T(8,128)S(1)}, f32[7,8,8,128]{3,2,1,0:T(8,128)S(1)}, u32[]{:S(2)}, u32[]{:S(2)}) collective-permute-start(f32[7,8,8,128]{3,2,1,0:T(8,128)S(1)} %get-tuple-element.50), channel_id=1, source_target_pairs={{64,128},{128,64},{192,256},{256,192},{320,384},{384,320},{65,129}... | collective-permute-start | bytes 688136 | tf_op jit(solution)/shard_map/ppermute | solution.py:217
  51.5 2.2 %collective-permute-start.10 = (f32[7,2,8,128]{3,2,1,0:T(8,128)S(1)}, f32[7,2,8,128]{3,2,1,0:T(8,128)S(1)}, u32[]{:S(2)}, u32[]{:S(2)}) collective-permute-start(f32[7,2,8,128]{3,2,1,0:T(8,128)S(1)} %get-tuple-element.52), channel_id=1, source_target_pairs={{0,8},{8,0},{16,24},{24,16},{32,40},{40,32},{48,56},{56,48},{1,9},... | collective-permute-start | bytes 172040 | tf_op jit(solution)/shard_map/ppermute | solution.py:219
  53.6 4.9 %collective-permute-start.11 = (f32[7,2,8,128]{3,2,1,0:T(8,128)S(1)}, f32[7,2,8,128]{3,2,1,0:T(8,128)S(1)}, u32[]{:S(2)}, u32[]{:S(2)}) collective-permute-start(f32[7,2,8,128]{3,2,1,0:T(8,128)S(1)} %get-tuple-element.53), channel_id=1, source_target_pairs={{0,56},{8,16},{16,8},{24,32},{32,24},{40,48},{48,40},{56,0},{1,57}... | collective-permute-start | bytes 172040 | tf_op jit(solution)/shard_map/ppermute | solution.py:220
  61.5 3.5 %collective-permute-start.12 = (f32[7,8,8,128]{3,2,1,0:T(8,128)S(1)}, f32[7,8,8,128]{3,2,1,0:T(8,128)S(1)}, u32[]{:S(2)}, u32[]{:S(2)}) collective-permute-start(f32[7,8,8,128]{3,2,1,0:T(8,128)S(1)} %get-tuple-element.55), channel_id=1, source_target_pairs={{64,128},{128,64},{192,256},{256,192},{320,384},{384,320},{65,129}... | collective-permute-start | bytes 688136 | tf_op jit(solution)/shard_map/ppermute | solution.py:217
  68.8 4.7 %collective-permute-start.15 = (f32[7,2,8,128]{3,2,1,0:T(8,128)S(1)}, f32[7,2,8,128]{3,2,1,0:T(8,128)S(1)}, u32[]{:S(2)}, u32[]{:S(2)}) collective-permute-start(f32[7,2,8,128]{3,2,1,0:T(8,128)S(1)} %get-tuple-element.58), channel_id=1, source_target_pairs={{0,56},{8,16},{16,8},{24,32},{32,24},{40,48},{48,40},{56,0},{1,57}... | collective-permute-start | bytes 172040 | tf_op jit(solution)/shard_map/ppermute | solution.py:220
  76.2 3.4 %collective-permute-start.16 = (f32[7,8,8,128]{3,2,1,0:T(8,128)S(1)}, f32[7,8,8,128]{3,2,1,0:T(8,128)S(1)}, u32[]{:S(2)}, u32[]{:S(2)}) collective-permute-start(f32[7,8,8,128]{3,2,1,0:T(8,128)S(1)} %get-tuple-element.61), channel_id=1, source_target_pairs={{64,128},{128,64},{192,256},{256,192},{320,384},{384,320},{65,129}... | collective-permute-start | bytes 688136 | tf_op jit(solution)/shard_map/ppermute | solution.py:217
  79.6 1.9 %collective-permute-start.17 = (f32[7,8,8,128]{3,2,1,0:T(8,128)S(1)}, f32[7,8,8,128]{3,2,1,0:T(8,128)S(1)}, u32[]{:S(2)}, u32[]{:S(2)}) collective-permute-start(f32[7,8,8,128]{3,2,1,0:T(8,128)S(1)} %get-tuple-element.62), channel_id=1, source_target_pairs={{0,64},{64,0},{128,192},{192,128},{256,320},{320,256},{384,448},{4... | collective-permute-start | bytes 688136 | tf_op jit(solution)/shard_map/ppermute | solution.py:218
  81.5 2.2 %collective-permute-start.18 = (f32[7,2,8,128]{3,2,1,0:T(8,128)S(1)}, f32[7,2,8,128]{3,2,1,0:T(8,128)S(1)}, u32[]{:S(2)}, u32[]{:S(2)}) collective-permute-start(f32[7,2,8,128]{3,2,1,0:T(8,128)S(1)} %get-tuple-element.63), channel_id=1, source_target_pairs={{0,8},{8,0},{16,24},{24,16},{32,40},{40,32},{48,56},{56,48},{1,9},... | collective-permute-start | bytes 172040 | tf_op jit(solution)/shard_map/ppermute | solution.py:219
  83.7 4.6 %collective-permute-start.19 = (f32[7,2,8,128]{3,2,1,0:T(8,128)S(1)}, f32[7,2,8,128]{3,2,1,0:T(8,128)S(1)}, u32[]{:S(2)}, u32[]{:S(2)}) collective-permute-start(f32[7,2,8,128]{3,2,1,0:T(8,128)S(1)} %get-tuple-element.64), channel_id=1, source_target_pairs={{0,56},{8,16},{16,8},{24,32},{32,24},{40,48},{48,40},{56,0},{1,57}... | collective-permute-start | bytes 172040 | tf_op jit(solution)/shard_map/ppermute | solution.py:220
  91.0 3.8 %collective-permute-start.20 = (f32[7,8,8,128]{3,2,1,0:T(8,128)S(1)}, f32[7,8,8,128]{3,2,1,0:T(8,128)S(1)}, u32[]{:S(2)}, u32[]{:S(2)}) collective-permute-start(f32[7,8,8,128]{3,2,1,0:T(8,128)S(1)} %get-tuple-element.66), channel_id=1, source_target_pairs={{64,128},{128,64},{192,256},{256,192},{320,384},{384,320},{65,129}... | collective-permute-start | bytes 688136 | tf_op jit(solution)/shard_map/ppermute | solution.py:217
  94.9 1.9 %collective-permute-start.21 = (f32[7,8,8,128]{3,2,1,0:T(8,128)S(1)}, f32[7,8,8,128]{3,2,1,0:T(8,128)S(1)}, u32[]{:S(2)}, u32[]{:S(2)}) collective-permute-start(f32[7,8,8,128]{3,2,1,0:T(8,128)S(1)} %get-tuple-element.67), channel_id=1, source_target_pairs={{0,64},{64,0},{128,192},{192,128},{256,320},{320,256},{384,448},{4... | collective-permute-start | bytes 688136 | tf_op jit(solution)/shard_map/ppermute | solution.py:218
  96.8 1.9 %collective-permute-start.22 = (f32[7,2,8,128]{3,2,1,0:T(8,128)S(1)}, f32[7,2,8,128]{3,2,1,0:T(8,128)S(1)}, u32[]{:S(2)}, u32[]{:S(2)}) collective-permute-start(f32[7,2,8,128]{3,2,1,0:T(8,128)S(1)} %get-tuple-element.68), channel_id=1, source_target_pairs={{0,8},{8,0},{16,24},{24,16},{32,40},{40,32},{48,56},{56,48},{1,9},... | collective-permute-start | bytes 172040 | tf_op jit(solution)/shard_map/ppermute | solution.py:219
  98.7 4.6 %collective-permute-start.23 = (f32[7,2,8,128]{3,2,1,0:T(8,128)S(1)}, f32[7,2,8,128]{3,2,1,0:T(8,128)S(1)}, u32[]{:S(2)}, u32[]{:S(2)}) collective-permute-start(f32[7,2,8,128]{3,2,1,0:T(8,128)S(1)} %get-tuple-element.69), channel_id=1, source_target_pairs={{0,56},{8,16},{16,8},{24,32},{32,24},{40,48},{48,40},{56,0},{1,57}... | collective-permute-start | bytes 172040 | tf_op jit(solution)/shard_map/ppermute | solution.py:220
  104.9 2.1 %last.1 = (f32[896,128]{1,0:T(8,128)}, f32[8,8,1792]{2,1,0:T(8,128)S(1)}) custom-call(f32[7,2,8,8,128]{4,3,2,1,0:T(8,128)S(1)} %get-tuple-element.65.fluxin, f32[7,8,8,128]{3,2,1,0:T(8,128)S(1)} %collective-permute-done.20.rcross, f32[7,8,8,128]{3,2,1,0:T(8,128)S(1)} %collective-permute-done.21.rinside, f32[7,2,8,128]{3,2,1,0:T(8,128)S(1)} %collective-permute-done.22.rya, ...), custom_call_target="tpu_custom_call" | custom-call | tf_op jit(solution)/shard_map/last/pallas_call | solution.py:192
  107.0 19.7 %all_to_all.20 = f32[8,8,1792]{2,1,0:T(8,128)S(1)} all-to-all(f32[8,8,1792]{2,1,0:T(8,128)S(1)} %get-tuple-element.71), channel_id=1, replica_groups=mesh['sx'=8,'sy'=8,'dir'=8] {'dir'}, dimensions={0} | all-to-all | bytes 917504 | tf_op jit(solution)/shard_map/all_to_all | solution.py:247
  127.2 11.6 %all_to_all.21.parts = f32[8,32,128]{2,1,0:T(8,128)S(1)} all-to-all(f32[8,32,128]{2,1,0:T(8,128)S(1)} %gram.1), channel_id=1, replica_groups=mesh['sx'=8,'sy'=8,'dir'=8] {'sx'}, dimensions={0} | all-to-all | bytes 262144 | tf_op jit(solution)/shard_map/all_to_all | solution.py:251
  138.8 12.5 %all_to_all.22.parts = f32[8,32,128]{2,1,0:T(8,128)S(1)} all-to-all(f32[8,32,128]{2,1,0:T(8,128)S(1)} %reduce_sx.1), channel_id=1, replica_groups=mesh['sx'=8,'sy'=8,'dir'=8] {'sy'}, dimensions={0} | all-to-all | bytes 262144 | tf_op jit(solution)/shard_map/all_to_all | solution.py:253
  151.3 10.4 %all_to_all.23.parts = f32[8,32,128]{2,1,0:T(8,128)S(1)} all-to-all(f32[8,32,128]{2,1,0:T(8,128)S(1)} %reduce_sy.1), channel_id=1, replica_groups=mesh['sx'=8,'sy'=8,'dir'=8] {'dir'}, dimensions={0} | all-to-all | bytes 262144 | tf_op jit(solution)/shard_map/all_to_all | solution.py:255
  161.9 5.8 %cholesky.18 = f32[64,64]{1,0:T(8,128)S(1)} custom-call(f32[64,64]{1,0:T(8,128)S(1)} %fusion), custom_call_target="Cholesky" | custom-call | tf_op jit(solution)/shard_map/jit(cholesky)/cholesky | solution.py:257
  (64 shorter events, 36.0 us)
Async XLA Ops:
  7.1 20.9 %collective-permute-start = (f32[7,8,8,128]{3,2,1,0:T(8,128)S(1)}, f32[7,8,8,128]{3,2,1,0:T(8,128)S(1)}, u32[]{:S(2)}, u32[]{:S(2)}) collective-permute-start(f32[7,8,8,128]{3,2,1,0:T(8,128)S(1)} %get-tuple-element.38), channel_id=1, source_target_pairs={{64,128},{128,64},{192,256},{256,192},{320,384},{384,320},{65,129}... | collective-permute-start | bytes 688136 | tf_op jit(solution)/shard_map/ppermute | solution.py:217
  11.6 16.4 %collective-permute-start.1 = (f32[7,8,8,128]{3,2,1,0:T(8,128)S(1)}, f32[7,8,8,128]{3,2,1,0:T(8,128)S(1)}, u32[]{:S(2)}, u32[]{:S(2)}) collective-permute-start(f32[7,8,8,128]{3,2,1,0:T(8,128)S(1)} %get-tuple-element.39), channel_id=1, source_target_pairs={{0,64},{64,0},{128,192},{192,128},{256,320},{320,256},{384,448},{4... | collective-permute-start | bytes 688136 | tf_op jit(solution)/shard_map/ppermute | solution.py:218
  16.5 9.9 %collective-permute-start.2 = (f32[7,2,8,128]{3,2,1,0:T(8,128)S(1)}, f32[7,2,8,128]{3,2,1,0:T(8,128)S(1)}, u32[]{:S(2)}, u32[]{:S(2)}) collective-permute-start(f32[7,2,8,128]{3,2,1,0:T(8,128)S(1)} %get-tuple-element.40), channel_id=1, source_target_pairs={{0,8},{8,0},{16,24},{24,16},{32,40},{40,32},{48,56},{56,48},{1,9},... | collective-permute-start | bytes 172040 | tf_op jit(solution)/shard_map/ppermute | solution.py:219
  18.5 9.5 %collective-permute-start.3 = (f32[7,2,8,128]{3,2,1,0:T(8,128)S(1)}, f32[7,2,8,128]{3,2,1,0:T(8,128)S(1)}, u32[]{:S(2)}, u32[]{:S(2)}) collective-permute-start(f32[7,2,8,128]{3,2,1,0:T(8,128)S(1)} %get-tuple-element.41), channel_id=1, source_target_pairs={{0,56},{8,16},{16,8},{24,32},{32,24},{40,48},{48,40},{56,0},{1,57}... | collective-permute-start | bytes 172040 | tf_op jit(solution)/shard_map/ppermute | solution.py:220
  29.1 14.9 %collective-permute-start.4 = (f32[7,8,8,128]{3,2,1,0:T(8,128)S(1)}, f32[7,8,8,128]{3,2,1,0:T(8,128)S(1)}, u32[]{:S(2)}, u32[]{:S(2)}) collective-permute-start(f32[7,8,8,128]{3,2,1,0:T(8,128)S(1)} %get-tuple-element.45), channel_id=1, source_target_pairs={{64,128},{128,64},{192,256},{256,192},{320,384},{384,320},{65,129}... | collective-permute-start | bytes 688136 | tf_op jit(solution)/shard_map/ppermute | solution.py:217
  33.8 10.3 %collective-permute-start.5 = (f32[7,8,8,128]{3,2,1,0:T(8,128)S(1)}, f32[7,8,8,128]{3,2,1,0:T(8,128)S(1)}, u32[]{:S(2)}, u32[]{:S(2)}) collective-permute-start(f32[7,8,8,128]{3,2,1,0:T(8,128)S(1)} %get-tuple-element.46), channel_id=1, source_target_pairs={{0,64},{64,0},{128,192},{192,128},{256,320},{320,256},{384,448},{4... | collective-permute-start | bytes 688136 | tf_op jit(solution)/shard_map/ppermute | solution.py:218
  35.7 6.8 %collective-permute-start.6 = (f32[7,2,8,128]{3,2,1,0:T(8,128)S(1)}, f32[7,2,8,128]{3,2,1,0:T(8,128)S(1)}, u32[]{:S(2)}, u32[]{:S(2)}) collective-permute-start(f32[7,2,8,128]{3,2,1,0:T(8,128)S(1)} %get-tuple-element.47), channel_id=1, source_target_pairs={{0,8},{8,0},{16,24},{24,16},{32,40},{40,32},{48,56},{56,48},{1,9},... | collective-permute-start | bytes 172040 | tf_op jit(solution)/shard_map/ppermute | solution.py:219
  37.6 6.4 %collective-permute-start.7 = (f32[7,2,8,128]{3,2,1,0:T(8,128)S(1)}, f32[7,2,8,128]{3,2,1,0:T(8,128)S(1)}, u32[]{:S(2)}, u32[]{:S(2)}) collective-permute-start(f32[7,2,8,128]{3,2,1,0:T(8,128)S(1)} %get-tuple-element.48), channel_id=1, source_target_pairs={{0,56},{8,16},{16,8},{24,32},{32,24},{40,48},{48,40},{56,0},{1,57}... | collective-permute-start | bytes 172040 | tf_op jit(solution)/shard_map/ppermute | solution.py:220
  45.2 14.9 %collective-permute-start.8 = (f32[7,8,8,128]{3,2,1,0:T(8,128)S(1)}, f32[7,8,8,128]{3,2,1,0:T(8,128)S(1)}, u32[]{:S(2)}, u32[]{:S(2)}) collective-permute-start(f32[7,8,8,128]{3,2,1,0:T(8,128)S(1)} %get-tuple-element.50), channel_id=1, source_target_pairs={{64,128},{128,64},{192,256},{256,192},{320,384},{384,320},{65,129}... | collective-permute-start | bytes 688136 | tf_op jit(solution)/shard_map/ppermute | solution.py:217
  49.5 10.5 %collective-permute-start.9 = (f32[7,8,8,128]{3,2,1,0:T(8,128)S(1)}, f32[7,8,8,128]{3,2,1,0:T(8,128)S(1)}, u32[]{:S(2)}, u32[]{:S(2)}) collective-permute-start(f32[7,8,8,128]{3,2,1,0:T(8,128)S(1)} %get-tuple-element.51), channel_id=1, source_target_pairs={{0,64},{64,0},{128,192},{192,128},{256,320},{320,256},{384,448},{4... | collective-permute-start | bytes 688136 | tf_op jit(solution)/shard_map/ppermute | solution.py:218
  51.5 7.1 %collective-permute-start.10 = (f32[7,2,8,128]{3,2,1,0:T(8,128)S(1)}, f32[7,2,8,128]{3,2,1,0:T(8,128)S(1)}, u32[]{:S(2)}, u32[]{:S(2)}) collective-permute-start(f32[7,2,8,128]{3,2,1,0:T(8,128)S(1)} %get-tuple-element.52), channel_id=1, source_target_pairs={{0,8},{8,0},{16,24},{24,16},{32,40},{40,32},{48,56},{56,48},{1,9},... | collective-permute-start | bytes 172040 | tf_op jit(solution)/shard_map/ppermute | solution.py:219
  53.6 6.4 %collective-permute-start.11 = (f32[7,2,8,128]{3,2,1,0:T(8,128)S(1)}, f32[7,2,8,128]{3,2,1,0:T(8,128)S(1)}, u32[]{:S(2)}, u32[]{:S(2)}) collective-permute-start(f32[7,2,8,128]{3,2,1,0:T(8,128)S(1)} %get-tuple-element.53), channel_id=1, source_target_pairs={{0,56},{8,16},{16,8},{24,32},{32,24},{40,48},{48,40},{56,0},{1,57}... | collective-permute-start | bytes 172040 | tf_op jit(solution)/shard_map/ppermute | solution.py:220
  61.5 13.6 %collective-permute-start.12 = (f32[7,8,8,128]{3,2,1,0:T(8,128)S(1)}, f32[7,8,8,128]{3,2,1,0:T(8,128)S(1)}, u32[]{:S(2)}, u32[]{:S(2)}) collective-permute-start(f32[7,8,8,128]{3,2,1,0:T(8,128)S(1)} %get-tuple-element.55), channel_id=1, source_target_pairs={{64,128},{128,64},{192,256},{256,192},{320,384},{384,320},{65,129}... | collective-permute-start | bytes 688136 | tf_op jit(solution)/shard_map/ppermute | solution.py:217
  64.9 10.1 %collective-permute-start.13 = (f32[7,8,8,128]{3,2,1,0:T(8,128)S(1)}, f32[7,8,8,128]{3,2,1,0:T(8,128)S(1)}, u32[]{:S(2)}, u32[]{:S(2)}) collective-permute-start(f32[7,8,8,128]{3,2,1,0:T(8,128)S(1)} %get-tuple-element.56), channel_id=1, source_target_pairs={{0,64},{64,0},{128,192},{192,128},{256,320},{320,256},{384,448},{4... | collective-permute-start | bytes 688136 | tf_op jit(solution)/shard_map/ppermute | solution.py:218
  66.9 6.6 %collective-permute-start.14 = (f32[7,2,8,128]{3,2,1,0:T(8,128)S(1)}, f32[7,2,8,128]{3,2,1,0:T(8,128)S(1)}, u32[]{:S(2)}, u32[]{:S(2)}) collective-permute-start(f32[7,2,8,128]{3,2,1,0:T(8,128)S(1)} %get-tuple-element.57), channel_id=1, source_target_pairs={{0,8},{8,0},{16,24},{24,16},{32,40},{40,32},{48,56},{56,48},{1,9},... | collective-permute-start | bytes 172040 | tf_op jit(solution)/shard_map/ppermute | solution.py:219
  68.8 6.3 %collective-permute-start.15 = (f32[7,2,8,128]{3,2,1,0:T(8,128)S(1)}, f32[7,2,8,128]{3,2,1,0:T(8,128)S(1)}, u32[]{:S(2)}, u32[]{:S(2)}) collective-permute-start(f32[7,2,8,128]{3,2,1,0:T(8,128)S(1)} %get-tuple-element.58), channel_id=1, source_target_pairs={{0,56},{8,16},{16,8},{24,32},{32,24},{40,48},{48,40},{56,0},{1,57}... | collective-permute-start | bytes 172040 | tf_op jit(solution)/shard_map/ppermute | solution.py:220
  76.2 13.6 %collective-permute-start.16 = (f32[7,8,8,128]{3,2,1,0:T(8,128)S(1)}, f32[7,8,8,128]{3,2,1,0:T(8,128)S(1)}, u32[]{:S(2)}, u32[]{:S(2)}) collective-permute-start(f32[7,8,8,128]{3,2,1,0:T(8,128)S(1)} %get-tuple-element.61), channel_id=1, source_target_pairs={{64,128},{128,64},{192,256},{256,192},{320,384},{384,320},{65,129}... | collective-permute-start | bytes 688136 | tf_op jit(solution)/shard_map/ppermute | solution.py:217
  79.6 10.2 %collective-permute-start.17 = (f32[7,8,8,128]{3,2,1,0:T(8,128)S(1)}, f32[7,8,8,128]{3,2,1,0:T(8,128)S(1)}, u32[]{:S(2)}, u32[]{:S(2)}) collective-permute-start(f32[7,8,8,128]{3,2,1,0:T(8,128)S(1)} %get-tuple-element.62), channel_id=1, source_target_pairs={{0,64},{64,0},{128,192},{192,128},{256,320},{320,256},{384,448},{4... | collective-permute-start | bytes 688136 | tf_op jit(solution)/shard_map/ppermute | solution.py:218
  81.5 6.7 %collective-permute-start.18 = (f32[7,2,8,128]{3,2,1,0:T(8,128)S(1)}, f32[7,2,8,128]{3,2,1,0:T(8,128)S(1)}, u32[]{:S(2)}, u32[]{:S(2)}) collective-permute-start(f32[7,2,8,128]{3,2,1,0:T(8,128)S(1)} %get-tuple-element.63), channel_id=1, source_target_pairs={{0,8},{8,0},{16,24},{24,16},{32,40},{40,32},{48,56},{56,48},{1,9},... | collective-permute-start | bytes 172040 | tf_op jit(solution)/shard_map/ppermute | solution.py:219
  83.7 6.1 %collective-permute-start.19 = (f32[7,2,8,128]{3,2,1,0:T(8,128)S(1)}, f32[7,2,8,128]{3,2,1,0:T(8,128)S(1)}, u32[]{:S(2)}, u32[]{:S(2)}) collective-permute-start(f32[7,2,8,128]{3,2,1,0:T(8,128)S(1)} %get-tuple-element.64), channel_id=1, source_target_pairs={{0,56},{8,16},{16,8},{24,32},{32,24},{40,48},{48,40},{56,0},{1,57}... | collective-permute-start | bytes 172040 | tf_op jit(solution)/shard_map/ppermute | solution.py:220
  91.0 13.8 %collective-permute-start.20 = (f32[7,8,8,128]{3,2,1,0:T(8,128)S(1)}, f32[7,8,8,128]{3,2,1,0:T(8,128)S(1)}, u32[]{:S(2)}, u32[]{:S(2)}) collective-permute-start(f32[7,8,8,128]{3,2,1,0:T(8,128)S(1)} %get-tuple-element.66), channel_id=1, source_target_pairs={{64,128},{128,64},{192,256},{256,192},{320,384},{384,320},{65,129}... | collective-permute-start | bytes 688136 | tf_op jit(solution)/shard_map/ppermute | solution.py:217
  94.9 10.0 %collective-permute-start.21 = (f32[7,8,8,128]{3,2,1,0:T(8,128)S(1)}, f32[7,8,8,128]{3,2,1,0:T(8,128)S(1)}, u32[]{:S(2)}, u32[]{:S(2)}) collective-permute-start(f32[7,8,8,128]{3,2,1,0:T(8,128)S(1)} %get-tuple-element.67), channel_id=1, source_target_pairs={{0,64},{64,0},{128,192},{192,128},{256,320},{320,256},{384,448},{4... | collective-permute-start | bytes 688136 | tf_op jit(solution)/shard_map/ppermute | solution.py:218
  96.8 6.5 %collective-permute-start.22 = (f32[7,2,8,128]{3,2,1,0:T(8,128)S(1)}, f32[7,2,8,128]{3,2,1,0:T(8,128)S(1)}, u32[]{:S(2)}, u32[]{:S(2)}) collective-permute-start(f32[7,2,8,128]{3,2,1,0:T(8,128)S(1)} %get-tuple-element.68), channel_id=1, source_target_pairs={{0,8},{8,0},{16,24},{24,16},{32,40},{40,32},{48,56},{56,48},{1,9},... | collective-permute-start | bytes 172040 | tf_op jit(solution)/shard_map/ppermute | solution.py:219
  98.7 6.1 %collective-permute-start.23 = (f32[7,2,8,128]{3,2,1,0:T(8,128)S(1)}, f32[7,2,8,128]{3,2,1,0:T(8,128)S(1)}, u32[]{:S(2)}, u32[]{:S(2)}) collective-permute-start(f32[7,2,8,128]{3,2,1,0:T(8,128)S(1)} %get-tuple-element.69), channel_id=1, source_target_pairs={{0,56},{8,16},{16,8},{24,32},{32,24},{40,48},{48,40},{56,0},{1,57}... | collective-permute-start | bytes 172040 | tf_op jit(solution)/shard_map/ppermute | solution.py:220
  (9 other events, 51.2 us)
